TPU v7x, 32 devices: a whole 2x2x4 slice. The times are simulated.
32 devices in a mesh: row: 4 (over y, x), col: 8 (over z, core).
Axes of the slice: x: 2, y: 2, z: 4, core: 2. Of those that a mesh axis runs over, the one named last changes fastest.
Arguments:
- latents: bfloat16 [1, 32, 32, 8192], P(None, 'col', None, 'row'), may hold values from -6 to 6
- kernel: bfloat16 [3, 3, 8192, 8192], P(None, None, 'row', 'col'), may hold values from -0.0234375 to 0.0234375
- out_grad: bfloat16 [1, 32, 32, 8192], P(None, 'row', None, 'col'), may hold values from -6 to 6
Outputs:
- conv_out: bfloat16 [1, 32, 32, 8192], P(None, 'row', None, 'col')
- latent_grad: bfloat16 [1, 32, 32, 8192], P(None, 'col', None, 'row')
All inputs are finite; a program needn't handle non-finite values.
Results may differ from a plain program's by a relative error of at most 0.001.
Values may be sent and summed in bfloat16 or wider, within the bound.
A program may use at most 192 MiB of HBM per device.

v0:
```python
import jax
import jax.numpy as jnp
from jax import lax
from jax.sharding import PartitionSpec as P


def conv_rows(padded, kernel, flip, count):
    frames = padded.shape[0]
    width = padded.shape[2] - 2
    chans = padded.shape[3]
    outer = kernel.shape[2] if flip else kernel.shape[3]
    total = jnp.zeros((frames * count * width, outer), jnp.float32)
    for tap_h in range(3):
        for tap_w in range(3):
            piece = padded[:, tap_h : tap_h + count, tap_w : tap_w + width, :].reshape(-1, chans)
            if flip:
                block = kernel[2 - tap_h, 2 - tap_w]
                total = total + lax.dot_general(
                    piece, block, (((1,), (1,)), ((), ())), preferred_element_type=jnp.float32
                )
            else:
                total = total + jnp.dot(
                    piece, kernel[tap_h, tap_w], preferred_element_type=jnp.float32
                )
    return total.reshape(frames, count, width, outer)


def pad_field(field):
    return jnp.pad(field, ((0, 0), (1, 1), (1, 1), (0, 0)))


def fetch_cotangents(out_grad):
    return lax.all_gather(out_grad, "row", axis=1, tiled=True)


def body(latents, kernel, out_grad):
    grad_full = None
    latent_full = lax.all_gather(latents, "col", axis=1, tiled=True)
    latent_pad = pad_field(latent_full)
    height = latent_full.shape[1]
    partial_out = conv_rows(latent_pad, kernel, False, height)
    conv_out = lax.psum_scatter(partial_out, "row", scatter_dimension=1, tiled=True)
    grad_full = fetch_cotangents(out_grad)
    grad_pad = pad_field(grad_full)
    partial_in = conv_rows(grad_pad, kernel, True, height)
    latent_grad = lax.psum_scatter(partial_in, "col", scatter_dimension=1, tiled=True)
    return (conv_out.astype(jnp.bfloat16), latent_grad.astype(jnp.bfloat16))


def solution(mesh):
    in_specs = (
        P(None, "col", None, "row"),
        P(None, None, "row", "col"),
        P(None, "row", None, "col"),
    )
    out_specs = (P(None, "row", None, "col"), P(None, "col", None, "row"))
    return jax.shard_map(body, mesh=mesh, in_specs=in_specs, out_specs=out_specs, check_vma=False)
```

profile of v0, /device:TPU:0, one launch (start us, length us, event | category | flops | bytes accessed | tf_op | source)
XLA Modules:
  0.0 395.2 jit_solution(12370931776684096442)
XLA Ops:
  8.7 39.1 %all-gather.5.cloned.1.call-done = bf16[1,32,32,1024]{3,2,0,1:T(8,128)(2,1)} async-done(((bf16[1,8,32,1024]{3,2,0,1:T(8,128)(2,1)}), bf16[1,32,32,1024]{3,2,0,1:T(8,128)(2,1)}) %all-gather.5.cloned.1.call-update) | async-done | bytes 2097168 | tf_op jit(solution)/shard_map/all_gather | solution.py:33
  47.8 14.2 %pad_slice_fusion.8 = (bf16[1,32,32,1024]{3,2,0,1:T(8,128)(2,1)}, bf16[1,32,32,1024]{3,2,0,1:T(8,128)(2,1)}, bf16[1,32,32,1024]{3,2,0,1:T(8,128)(2,1)}, bf16[1,3...) fusion(bf16[1,32,32,1024]{3,2,0,1:T(8,128)(2,1)} %all-gather.5., ...), kind=kLoop, calls=%fused_computation.64 | loop fusion | bytes 18874368 | tf_op jit(solution)/shard_map/slice | solution.py:15
  61.9 9.0 %fusion = f32[1024,2048]{1,0:T(8,128)} fusion(bf16[1024,1024]{1,0:T(8,128)(2,1)S(1)} %bitcast.110, bf16[3,3,2048,1024]{3,2,1,0:T(8,128)(2,1)} %param.4), kind=kOutput, calls=%fused_computation.9 | convolution fusion | flops 4294967296 | bytes 14680064 | tf_op jit(solution)/shard_map/dot_general | solution.py:18
  71.0 9.1 %fusion.12 = f32[1024,2048]{1,0:T(8,128)} fusion(bf16[1024,1024]{1,0:T(8,128)(2,1)S(1)} %bitcast.109, bf16[3,3,2048,1024]{3,2,1,0:T(8,128)(2,1)} %param.4), kind=kOutput, calls=%fused_computation.21 | convolution fusion | flops 4294967296 | bytes 14680064 | tf_op jit(solution)/shard_map/dot_general | solution.py:18
  80.1 16.2 %all-gather.3.cloned.1.call-done = bf16[1,32,32,2048]{3,2,0,1:T(8,128)(2,1)} async-done(((bf16[1,4,32,2048]{3,2,0,1:T(8,128)(2,1)}), bf16[1,32,32,2048]{3,2,0,1:T(8,128)(2,1)}) %all-gather.3.cloned.1.call-update) | async-done | bytes 4194320 | tf_op jit(solution)/shard_map/all_gather | solution.py:38
  96.2 23.1 %pad_slice_fusion.7 = (bf16[1,32,32,2048]{3,2,0,1:T(8,128)(2,1)S(1)}, bf16[1,32,32,2048]{3,2,0,1:T(8,128)(2,1)S(1)}, bf16[1,32,32,2048]{3,2,0,1:T(8,128)(2,1)S(1...) fusion(bf16[1,32,32,2048]{3,2,0,1:T(8,128)(2,1)} %all-gather.3., ...), kind=kLoop, calls=%fused_computation.8 | loop fusion | bytes 37748736 | tf_op jit(solution)/shard_map/slice | solution.py:15
  119.4 10.1 %fusion.10 = f32[1024,1024]{1,0:T(8,128)} fusion(bf16[1024,2048]{1,0:T(8,128)(2,1)} %bitcast.102, bf16[3,3,2048,1024]{3,2,1,0:T(8,128)(2,1)} %param.4), kind=kOutput, calls=%fused_computation.19 | convolution fusion | flops 4294967296 | bytes 12582912 | tf_op jit(solution)/shard_map/dot_general | solution.py:22
  129.5 8.3 %fusion.14 = f32[1024,1024]{1,0:T(8,128)} fusion(bf16[1024,2048]{1,0:T(8,128)(2,1)S(1)} %bitcast.101, bf16[3,3,2048,1024]{3,2,1,0:T(8,128)(2,1)} %param.4), kind=kOutput, calls=%fused_computation.23 | convolution fusion | flops 4294967296 | bytes 12582912 | tf_op jit(solution)/shard_map/dot_general | solution.py:22
  137.8 8.3 %fusion.2 = f32[1024,1024]{1,0:T(8,128)} fusion(bf16[1024,2048]{1,0:T(8,128)(2,1)S(1)} %bitcast.100, bf16[3,3,2048,1024]{3,2,1,0:T(8,128)(2,1)} %param.4), kind=kOutput, calls=%fused_computation.11 | convolution fusion | flops 4294967296 | bytes 12582912 | tf_op jit(solution)/shard_map/dot_general | solution.py:22
  146.1 8.2 %fusion.22 = f32[1024,1024]{1,0:T(8,128)} fusion(bf16[1024,2048]{1,0:T(8,128)(2,1)S(1)} %bitcast.99, bf16[3,3,2048,1024]{3,2,1,0:T(8,128)(2,1)} %param.4), kind=kOutput, calls=%fused_computation.31 | convolution fusion | flops 4294967296 | bytes 12582912 | tf_op jit(solution)/shard_map/dot_general | solution.py:22
  154.4 8.3 %fusion.26 = f32[1024,1024]{1,0:T(8,128)} fusion(bf16[1024,2048]{1,0:T(8,128)(2,1)S(1)} %bitcast.98, bf16[3,3,2048,1024]{3,2,1,0:T(8,128)(2,1)} %param.4), kind=kOutput, calls=%fused_computation.35 | convolution fusion | flops 4294967296 | bytes 12582912 | tf_op jit(solution)/shard_map/dot_general | solution.py:22
  162.7 8.2 %fusion.30 = f32[1024,1024]{1,0:T(8,128)} fusion(bf16[1024,2048]{1,0:T(8,128)(2,1)S(1)} %bitcast.97, bf16[3,3,2048,1024]{3,2,1,0:T(8,128)(2,1)} %param.4), kind=kOutput, calls=%fused_computation.39 | convolution fusion | flops 4294967296 | bytes 12582912 | tf_op jit(solution)/shard_map/dot_general | solution.py:22
  170.9 19.3 %fusion.6 = f32[1024,1024]{1,0:T(8,128)} fusion(bf16[1024,2048]{1,0:T(8,128)(2,1)S(1)} %bitcast.96, bf16[3,3,2048,1024]{3,2,1,0:T(8,128)(2,1)} %param.4), kind=kOutput, calls=%fused_computation.15 | convolution fusion | flops 4294967296 | bytes 12582912 | tf_op jit(solution)/shard_map/dot_general | solution.py:22
  190.2 8.2 %fusion.18 = f32[1024,1024]{1,0:T(8,128)} fusion(bf16[1024,2048]{1,0:T(8,128)(2,1)S(1)} %bitcast.95, bf16[3,3,2048,1024]{3,2,1,0:T(8,128)(2,1)} %param.4), kind=kOutput, calls=%fused_computation.27 | convolution fusion | flops 4294967296 | bytes 12582912 | tf_op jit(solution)/shard_map/dot_general | solution.py:22
  198.4 16.0 %add_add_fusion.1 = f32[1024,1024]{1,0:T(8,128)} fusion(f32[1024,1024]{1,0:T(8,128)} %fusion.2, f32[1024,1024]{1,0:T(8,128)} %fusion.6, f32[1024,1024]{1,0:T(8,128)} %fusion.10, f32[1024,1024]{1,0:T(8,128)} %fusion.14, f32[1024,1024]{1,0:T(8,128)} %fusion.18, f32[1024,1024]{1,0:T(8,128)} %fusion.22, f32[1024,1024]{1,0:T(8,128)} %fusion.26, ...), kind=kOutput, calls=%fused_computation.45 | convolution fusion | flops 4303355904 | bytes 46137344 | tf_op jit(solution)/shard_map/dot_general | solution.py:22
  216.0 9.1 %fusion.20 = f32[1024,2048]{1,0:T(8,128)} fusion(bf16[1024,1024]{1,0:T(8,128)(2,1)S(1)} %bitcast.108, bf16[3,3,2048,1024]{3,2,1,0:T(8,128)(2,1)} %param.4), kind=kOutput, calls=%fused_computation.29 | convolution fusion | flops 4294967296 | bytes 14680064 | tf_op jit(solution)/shard_map/dot_general | solution.py:18
  225.1 9.3 %fusion.24 = f32[1024,2048]{1,0:T(8,128)} fusion(bf16[1024,1024]{1,0:T(8,128)(2,1)S(1)} %bitcast.107, bf16[3,3,2048,1024]{3,2,1,0:T(8,128)(2,1)} %param.4), kind=kOutput, calls=%fused_computation.33 | convolution fusion | flops 4294967296 | bytes 14680064 | tf_op jit(solution)/shard_map/dot_general | solution.py:18
  234.4 9.2 %fusion.28 = f32[1024,2048]{1,0:T(8,128)} fusion(bf16[1024,1024]{1,0:T(8,128)(2,1)S(1)} %bitcast.106, bf16[3,3,2048,1024]{3,2,1,0:T(8,128)(2,1)} %param.4), kind=kOutput, calls=%fused_computation.37 | convolution fusion | flops 4294967296 | bytes 14680064 | tf_op jit(solution)/shard_map/dot_general | solution.py:18
  243.6 9.1 %fusion.4 = f32[1024,2048]{1,0:T(8,128)} fusion(bf16[1024,1024]{1,0:T(8,128)(2,1)S(1)} %bitcast.105, bf16[3,3,2048,1024]{3,2,1,0:T(8,128)(2,1)} %param.4), kind=kOutput, calls=%fused_computation.13 | convolution fusion | flops 4294967296 | bytes 14680064 | tf_op jit(solution)/shard_map/dot_general | solution.py:18
  252.7 9.0 %fusion.8 = f32[1024,2048]{1,0:T(8,128)} fusion(bf16[1024,1024]{1,0:T(8,128)(2,1)S(1)} %bitcast.104, bf16[3,3,2048,1024]{3,2,1,0:T(8,128)(2,1)} %param.4), kind=kOutput, calls=%fused_computation.17 | convolution fusion | flops 4294967296 | bytes 14680064 | tf_op jit(solution)/shard_map/dot_general | solution.py:18
  261.8 9.4 %fusion.16 = f32[1024,2048]{1,0:T(8,128)} fusion(bf16[1024,1024]{1,0:T(8,128)(2,1)S(1)} %bitcast.103, bf16[3,3,2048,1024]{3,2,1,0:T(8,128)(2,1)} %param.4), kind=kOutput, calls=%fused_computation.25 | convolution fusion | flops 4294967296 | bytes 14680064 | tf_op jit(solution)/shard_map/dot_general | solution.py:18
  271.2 26.1 %add_add_fusion = f32[1024,2048]{1,0:T(8,128)} fusion(f32[1024,2048]{1,0:T(8,128)} %fusion.28, f32[1024,2048]{1,0:T(8,128)} %fusion.24, f32[1024,2048]{1,0:T(8,128)} %fusion.20, f32[1024,2048]{1,0:T(8,128)} %fusion.16, f32[1024,2048]{1,0:T(8,128)} %fusion.12, f32[1024,2048]{1,0:T(8,128)} %fusion.8, f32[1024,2048]{1,0:T(8,128)S(1)} %bitcast.93, ...), kind=kOutput, calls=%fused_computation | convolution fusion | flops 4311744512 | bytes 81788928 | tf_op jit(solution)/shard_map/dot_general | solution.py:18
  297.4 2.1 convert_element_type.10
  299.5 86.8 %reduce-scatter.5.cloned.1.call-done = f32[1,4,32,2048]{3,2,1,0:T(8,128)} async-done(((f32[1,32,32,2048]{3,2,1,0:T(8,128)}), f32[1,4,32,2048]{3,2,1,0:T(8,128)}) %reduce-scatter.5.cloned.1.call-update) | async-done | bytes 1048592 | tf_op jit(solution)/shard_map/reduce_scatter | solution.py:46
  (37 shorter events, 5.2 us)
Async XLA Ops:
  7.2 40.6 %all-gather.5.cloned.1.call-start = ((), (), s32[]{:S(2)}) async-start(), calls=%async_computation.4 | async-start | bytes 2621440 | tf_op jit(solution)/shard_map/all_gather | solution.py:33
  7.9 88.3 %all-gather.3.cloned.1.call-start = ((), (), s32[]{:S(2)}) async-start(), calls=%async_computation.2 | async-start | bytes 4718592 | tf_op jit(solution)/shard_map/all_gather | solution.py:38
  8.6 288.8 %reduce-scatter.3.cloned.1.call-start = ((), (), s32[]{:S(2)}) async-start(), calls=%async_computation.3 | async-start | bytes 5242880 | tf_op jit(solution)/shard_map/reduce_scatter | solution.py:42
  119.4 10.1 %copy-start.4 = (bf16[1,32,32,2048]{3,2,0,1:T(8,128)(2,1)S(1)}, bf16[1,32,32,2048]{3,2,0,1:T(8,128)(2,1)}, u32[]{:S(2)}) copy-start(bf16[1,32,32,2048]{3,2,0,1:T(8,128)(2,1)} %get-tuple-element.6) | copy-start | bytes 12582916
  129.5 8.3 %copy-start.3 = (bf16[1,32,32,2048]{3,2,0,1:T(8,128)(2,1)S(1)}, bf16[1,32,32,2048]{3,2,0,1:T(8,128)(2,1)}, u32[]{:S(2)}) copy-start(bf16[1,32,32,2048]{3,2,0,1:T(8,128)(2,1)} %get-tuple-element.9) | copy-start | bytes 12582916
  137.8 8.3 %copy-start.2 = (bf16[1,32,32,2048]{3,2,0,1:T(8,128)(2,1)S(1)}, bf16[1,32,32,2048]{3,2,0,1:T(8,128)(2,1)}, u32[]{:S(2)}) copy-start(bf16[1,32,32,2048]{3,2,0,1:T(8,128)(2,1)} %get-tuple-element.5) | copy-start | bytes 12582916
  170.9 19.3 %copy-start.1 = (bf16[1,32,32,2048]{3,2,0,1:T(8,128)(2,1)S(1)}, bf16[1,32,32,2048]{3,2,0,1:T(8,128)(2,1)}, u32[]{:S(2)}) copy-start(bf16[1,32,32,2048]{3,2,0,1:T(8,128)(2,1)} %all-gather.3.cloned.1.call-done) | copy-start | bytes 12582916
  214.4 1.6 copy-start.10
  214.4 171.9 %reduce-scatter.5.cloned.1.call-start = ((), (), s32[]{:S(2)}) async-start(), calls=%async_computation.5 | async-start | bytes 9437184 | tf_op jit(solution)/shard_map/reduce_scatter | solution.py:46
  216.0 9.1 %copy-start.9 = (bf16[1,32,32,1024]{3,2,0,1:T(8,128)(2,1)S(1)}, bf16[1,32,32,1024]{3,2,0,1:T(8,128)(2,1)}, u32[]{:S(2)}) copy-start(bf16[1,32,32,1024]{3,2,0,1:T(8,128)(2,1)} %get-tuple-element.15) | copy-start | bytes 6291460
  225.1 9.3 %copy-start.8 = (bf16[1,32,32,1024]{3,2,0,1:T(8,128)(2,1)S(1)}, bf16[1,32,32,1024]{3,2,0,1:T(8,128)(2,1)}, u32[]{:S(2)}) copy-start(bf16[1,32,32,1024]{3,2,0,1:T(8,128)(2,1)} %get-tuple-element.16) | copy-start | bytes 6291460
  234.4 9.2 %copy-start.7 = (bf16[1,32,32,1024]{3,2,0,1:T(8,128)(2,1)S(1)}, bf16[1,32,32,1024]{3,2,0,1:T(8,128)(2,1)}, u32[]{:S(2)}) copy-start(bf16[1,32,32,1024]{3,2,0,1:T(8,128)(2,1)} %get-tuple-element.11) | copy-start | bytes 6291460
  243.6 9.1 %copy-start.6 = (bf16[1,32,32,1024]{3,2,0,1:T(8,128)(2,1)S(1)}, bf16[1,32,32,1024]{3,2,0,1:T(8,128)(2,1)}, u32[]{:S(2)}) copy-start(bf16[1,32,32,1024]{3,2,0,1:T(8,128)(2,1)} %get-tuple-element.12) | copy-start | bytes 6291460
  252.7 9.0 %copy-start.5 = (bf16[1,32,32,1024]{3,2,0,1:T(8,128)(2,1)S(1)}, bf16[1,32,32,1024]{3,2,0,1:T(8,128)(2,1)}, u32[]{:S(2)}) copy-start(bf16[1,32,32,1024]{3,2,0,1:T(8,128)(2,1)} %all-gather.5.cloned.1.call-done) | copy-start | bytes 6291460
  261.8 9.4 %slice-start = ((s8[8388608]{0:T(1024)(128)(4,1)}), s8[4194304]{0:T(1024)(128)(4,1)S(1)}, s32[]{:S(2)}) async-start(s8[8388608]{0:T(1024)(128)(4,1)} %bitcast.92), calls=%async_computation.6 | async-start | bytes 8388608
  261.8 9.4 %slice-start.1 = ((s8[8388608]{0:T(1024)(128)(4,1)}), s8[4194304]{0:T(1024)(128)(4,1)S(1)}, s32[]{:S(2)}) async-start(s8[8388608]{0:T(1024)(128)(4,1)} %bitcast.92), calls=%async_computation.7 | async-start | bytes 8388608
  261.8 9.4 %copy-start = (bf16[1,32,32,1024]{3,2,0,1:T(8,128)(2,1)S(1)}, bf16[1,32,32,1024]{3,2,0,1:T(8,128)(2,1)}, u32[]{:S(2)}) copy-start(bf16[1,32,32,1024]{3,2,0,1:T(8,128)(2,1)} %get-tuple-element.10) | copy-start | bytes 6291460
Sparse Core Ops, SparseCore 0:
  9.8 37.8 all-gather.4
  49.3 46.8 all-gather.2
  214.6 51.3 reduce-scatter.2
  297.5 88.7 reduce-scatter.4
where the time goes:
time: 398 us; the launch traced here: 395 us
  matrix products  194 us (49%)
  waiting for transfers between devices  144 us (36%)
  local copies, waits for them, and re-layouts  38.8 us (10%)
  between operations  14.1 us (4%)
  other arithmetic  4.18 us (1%)
    dot_general x9, matrix products, conv_rows(): lax.dot_general(piece, block, (((1,), (1,)), ((), ())), preferred_element...  99.4 us
    dot_general x9, matrix products, conv_rows(): jnp.dot(piece, kernel[tap_h, tap_w], preferred_element_type=jnp.float32)  95 us
    reduce_scatter x1, waiting for transfers between devices, body(): lax.psum_scatter(partial_in, 'col', scatter_dimension=1, tiled=True)  86.8 us
    all_gather x1, waiting for transfers between devices, fetch_cotangents(): return lax.all_gather(out_grad, 'row', axis=1, tiled=True)  39.1 us
    slice x2, local copies, waits for them, and re-layouts, conv_rows(): padded[:, tap_h:tap_h + count, tap_w:tap_w + width, :].reshape(-1, chans)  37.3 us
    all_gather x1, waiting for transfers between devices, body(): latent_full = lax.all_gather(latents, 'col', axis=1, tiled=True)  16.2 us
  transfers between devices with their start and end apart: 4, of which 3 were waited for; matrix products, arithmetic and copies ran while one was open for 29% of the time, Pallas kernels for 0%

commit v1 on v0

v1 whole, which is shorter than its diff:
```python
import functools

import jax
import jax.numpy as jnp
from jax import lax
from jax.experimental import pallas as pl
from jax.experimental.pallas import tpu as pltpu
from jax.sharding import PartitionSpec as P

MESH = pl.DeviceIdType.MESH
SLOTS = 4


def dot_nn(a, b):
    return jnp.dot(a, b, preferred_element_type=jnp.float32)


def dot_nt(a, b):
    return lax.dot_general(a, b, (((1,), (1,)), ((), ())), preferred_element_type=jnp.float32)


def kernel(cfg, lat, ker, og, conv, lgrad, gpad, xpad, acc, wb, wf, bp, pr, zr, fp, fr,
           wbs, wfs, loc, ogs, ogr, las, lar, prs, prr, zrs, zrr, frs, frr):
    R, C, W, M, rw, cw, ci, co, tb, tf = cfg
    nb, nf, nz = ci // tb, co // tf, C // 2
    r = lax.axis_index("row")
    c = lax.axis_index("col")
    z, me = c // 2, c % 2
    other = 1 - me

    def fetch_b(s):
        t, kw, kh = s // 9, (s % 9) // 3, s % 3
        return pltpu.make_async_copy(
            ker.at[kh, kw, pl.ds(pl.multiple_of(t * tb, tb), tb), :], wb.at[s % SLOTS], wbs.at[s % SLOTS])

    def fetch_f(s):
        t, kw, kh = s // 9, (s % 9) // 3, s % 3
        return pltpu.make_async_copy(
            ker.at[kh, kw, :, pl.ds(pl.multiple_of(t * tf, tf), tf)], wf.at[s % SLOTS], wfs.at[s % SLOTS])

    for s in range(SLOTS - 1):
        fetch_b(s).start()
        fetch_f(s).start()

    def g_block(k):
        return gpad.at[pl.ds(pl.multiple_of(W + k * rw, W), rw), :]

    def x_block(k):
        return xpad.at[pl.ds(pl.multiple_of(W + k * cw, W), cw), :]

    own_g = pltpu.make_async_copy(og, g_block(r), loc.at[0])
    own_x = pltpu.make_async_copy(lat, x_block(c), loc.at[1])
    own_g.start()
    own_x.start()

    barrier = pltpu.get_barrier_semaphore()
    for d in range(1, R):
        pl.semaphore_signal(barrier, inc=1, device_id={"row": (r + d) % R}, device_id_type=MESH)
    for d in range(1, C):
        pl.semaphore_signal(barrier, inc=1, device_id={"col": (c + d) % C}, device_id_type=MESH)
    pl.semaphore_wait(barrier, R - 1 + C - 1)

    def send_g(d, k):
        return pltpu.make_async_remote_copy(
            src_ref=og, dst_ref=g_block(k), send_sem=ogs.at[d - 1], recv_sem=ogr.at[d - 1],
            device_id={"row": (r + d) % R}, device_id_type=MESH)

    def send_x(d, k):
        return pltpu.make_async_remote_copy(
            src_ref=lat, dst_ref=x_block(k), send_sem=las.at[d - 1], recv_sem=lar.at[d - 1],
            device_id={"col": (c + d) % C}, device_id_type=MESH)

    for d in range(1, R):
        send_g(d, r).start()
    for d in range(1, C):
        send_x(d, c).start()

    gpad[:W, :] = jnp.zeros((W, co), gpad.dtype)
    gpad[M + W :, :] = jnp.zeros((W, co), gpad.dtype)
    xpad[:W, :] = jnp.zeros((W, ci), xpad.dtype)
    xpad[M + W :, :] = jnp.zeros((W, ci), xpad.dtype)

    def send_pair(t):
        return pltpu.make_async_remote_copy(
            src_ref=bp.at[t, other], dst_ref=pr.at[t], send_sem=prs.at[t], recv_sem=prr.at[t],
            device_id={"col": z * 2 + other}, device_id_type=MESH)

    def send_z(t, d, slot):
        peer = (z + d) % nz
        return pltpu.make_async_remote_copy(
            src_ref=bp.at[t, me, peer], dst_ref=zr.at[t, slot], send_sem=zrs.at[t, d - 1],
            recv_sem=zrr.at[t, d - 1], device_id={"col": peer * 2 + me}, device_id_type=MESH)

    def send_r(t, d, slot):
        peer = (r + d) % R
        return pltpu.make_async_remote_copy(
            src_ref=fp.at[t, peer], dst_ref=fr.at[t, slot], send_sem=frs.at[t, d - 1],
            recv_sem=frr.at[t, d - 1], device_id={"row": peer}, device_id_type=MESH)

    def pair_sum(t):
        send_pair(t).wait_recv()

        def add(k, _):
            bp[t, me, k] = bp[t, me, k] + pr[t, k]
            return 0

        lax.fori_loop(0, nz, add, 0)
        for d in range(1, nz):
            send_z(t, d, z).start()

    def shifted(lo, n, first, last, cols):
        col = lax.broadcasted_iota(jnp.int32, (n, cols), 0) % W
        rows = pl.ds(pl.multiple_of(lo, n), n)
        down = pltpu.roll(acc[first, rows, :cols], 1, 0)
        up = pltpu.roll(acc[last, rows, :cols], n - 1, 0)
        return acc[1, rows, :cols] + jnp.where(col == 0, 0.0, down) + jnp.where(col == W - 1, 0.0, up)

    own_g.wait()
    for d in range(1, R):
        send_g(d, (r + R - d) % R).wait_recv()

    def taps(t, fetch, total, buf, dot, src, flip, cols):
        def step(kw, _):
            for kh in range(3):
                s = t * 9 + kw * 3 + kh
                fetch(s).wait()

                @pl.when(s + SLOTS - 1 < total)
                def _():
                    fetch(s + SLOTS - 1).start()

                top = (2 - kh) * W if flip else kh * W
                part = dot(src[top : top + M, :], buf[s % SLOTS])
                if kh == 0:
                    acc[kw, :, :cols] = part
                else:
                    acc[kw, :, :cols] += part
            return 0

        lax.fori_loop(0, 3, step, 0)

    def back(t, _):
        taps(t, fetch_b, nb * 9, wb, dot_nt, gpad, True, tb)

        def put(k, _):
            bp[t, k % 2, k // 2] = shifted(k * cw, cw, 2, 0, tb)
            return 0

        lax.fori_loop(0, C, put, 0)
        send_pair(t).start()

        @pl.when(t > 0)
        def _():
            pair_sum(t - 1)

        return 0

    lax.fori_loop(0, nb, back, 0)

    own_x.wait()
    for d in range(1, C):
        send_x(d, (c + C - d) % C).wait_recv()

    def fore(t, _):
        taps(t, fetch_f, nf * 9, wf, dot_nn, xpad, False, tf)

        def put(k, _):
            fp[t, k] = shifted(k * rw, rw, 0, 2, tf)
            return 0

        lax.fori_loop(0, R, put, 0)
        for d in range(1, R):
            send_r(t, d, r).start()

        @pl.when(t == 0)
        def _():
            pair_sum(nb - 1)

        return 0

    lax.fori_loop(0, nf, fore, 0)

    for d in range(1, R):
        send_g(d, r).wait_send()
    for d in range(1, C):
        send_x(d, c).wait_send()
    for t in range(nb):
        send_pair(t).wait_send()
        total = bp[t, me, z]
        for d in range(1, nz):
            src = (z + nz - d) % nz
            send_z(t, d, src).wait_recv()
            total = total + zr[t, src]
        lgrad[:, t * tb : (t + 1) * tb] = total.astype(lgrad.dtype)
        for d in range(1, nz):
            send_z(t, d, z).wait_send()
    for t in range(nf):
        total = fp[t, r]
        for d in range(1, R):
            src = (r + R - d) % R
            send_r(t, d, src).wait_recv()
            total = total + fr[t, src]
        conv[:, t * tf : (t + 1) * tf] = total.astype(conv.dtype)
        for d in range(1, R):
            send_r(t, d, r).wait_send()


def body(R, C, latents, kern, out_grad):
    _, hc, W, ci = latents.shape
    hr, co = out_grad.shape[1], out_grad.shape[3]
    M, rw, cw = hr * R * W, hr * W, hc * W
    tb, tf = min(512, ci), min(256, co)
    nb, nf, nz = ci // tb, co // tf, C // 2
    cfg = (R, C, W, M, rw, cw, ci, co, tb, tf)
    bf, f32 = jnp.bfloat16, jnp.float32
    dma = pltpu.SemaphoreType.DMA
    conv, lgrad = pl.pallas_call(
        functools.partial(kernel, cfg),
        out_shape=(jax.ShapeDtypeStruct((rw, co), bf), jax.ShapeDtypeStruct((cw, ci), bf)),
        in_specs=[pl.BlockSpec(memory_space=pl.ANY)] * 3,
        out_specs=(pl.BlockSpec(memory_space=pltpu.VMEM),) * 2,
        scratch_shapes=[
            pltpu.VMEM((M + 2 * W, co), bf),
            pltpu.VMEM((M + 2 * W, ci), bf),
            pltpu.VMEM((3, M, max(tb, tf)), f32),
            pltpu.VMEM((SLOTS, tb, co), bf),
            pltpu.VMEM((SLOTS, ci, tf), bf),
            pltpu.VMEM((nb, 2, nz, cw, tb), f32),
            pltpu.VMEM((nb, nz, cw, tb), f32),
            pltpu.VMEM((nb, nz, cw, tb), f32),
            pltpu.VMEM((nf, R, rw, tf), f32),
            pltpu.VMEM((nf, R, rw, tf), f32),
            dma((SLOTS,)), dma((SLOTS,)), dma((2,)),
            dma((R - 1,)), dma((R - 1,)),
            dma((C - 1,)), dma((C - 1,)),
            dma((nb,)), dma((nb,)),
            dma((nb, nz - 1)), dma((nb, nz - 1)),
            dma((nf, R - 1)), dma((nf, R - 1)),
        ],
        compiler_params=pltpu.CompilerParams(
            collective_id=0, has_side_effects=True, vmem_limit_bytes=66 * 1000 * 1000),
    )(latents.reshape(cw, ci), kern, out_grad.reshape(rw, co))
    return conv.reshape(1, hr, W, co), lgrad.reshape(1, hc, W, ci)


def solution(mesh):
    in_specs = (
        P(None, "col", None, "row"),
        P(None, None, "row", "col"),
        P(None, "row", None, "col"),
    )
    out_specs = (P(None, "row", None, "col"), P(None, "col", None, "row"))
    run = functools.partial(body, mesh.shape["row"], mesh.shape["col"])
    return jax.shard_map(run, mesh=mesh, in_specs=in_specs, out_specs=out_specs, check_vma=False)
```

time: 398 us -> 219 us (0.55)
  the two profiles are of different devices: /device:TPU:0 before, /device:TPU:9 now
where the time goes in v1:
time: 219 us
  Pallas kernels  214 us (98%)
  local copies, waits for them, and re-layouts  3.75 us (2%)
    pallas_call x1, Pallas kernels, body(): pl.pallas_call(functools.partial(kernel, cfg), out_shape=(jax.ShapeDtypeS...  214 us

profile of v1, /device:TPU:9, one launch (start us, length us, event | category | flops | bytes accessed | tf_op | source)
XLA Modules:
  0.0 218.8 jit_solution(15383883717385875223)
XLA Ops:
  0.6 214.4 %shard_map.50 = (bf16[256,1024]{1,0:T(8,128)(2,1)}, bf16[128,2048]{1,0:T(8,128)(2,1)}) custom-call(bf16[128,2048]{1,0:T(8,128)(2,1)} %bitcast.4, bf16[3,3,2048,1024]{3,2,1,0:T(8,128)(2,1)} %ker.1, bf16[256,1024]{1,0:T(8,128)(2,1)} %bitcast.5), custom_call_target="tpu_custom_call" | custom-call | tf_op jit(solution)/shard_map/pallas_call | solution.py:217
  215.0 1.9 copy.7
  216.9 1.9 copy.8

commit v2 on v1

--- a/solution.py
+++ b/solution.py
@@ -8,7 +8,7 @@
 from jax.sharding import PartitionSpec as P
 
 MESH = pl.DeviceIdType.MESH
-SLOTS = 4
+SLOTS = 6
 
 
 def dot_nn(a, b):
@@ -19,14 +19,17 @@
     return lax.dot_general(a, b, (((1,), (1,)), ((), ())), preferred_element_type=jnp.float32)
 
 
-def kernel(cfg, lat, ker, og, conv, lgrad, gpad, xpad, acc, wb, wf, bp, pr, zr, fp, fr,
-           wbs, wfs, loc, ogs, ogr, las, lar, prs, prr, zrs, zrr, frs, frr):
+def kernel(cfg, lat, ker, og, conv, lgrad, gpad, xpad, acc, wb, wf, bp, pr, qr, zr, fp, fr,
+           wbs, wfs, loc, ogs, ogr, las, lar, res, rer, prs, prr, qrs, qrr, zrs, zrr, frs, frr):
     R, C, W, M, rw, cw, ci, co, tb, tf = cfg
     nb, nf, nz = ci // tb, co // tf, C // 2
+    nq = nz // 2
     r = lax.axis_index("row")
     c = lax.axis_index("col")
     z, me = c // 2, c % 2
     other = 1 - me
+    q, zp = z // 2, z % 2
+    mate = 1 - zp
 
     def fetch_b(s):
         t, kw, kh = s // 9, (s % 9) // 3, s % 3
@@ -38,7 +41,7 @@
         return pltpu.make_async_copy(
             ker.at[kh, kw, :, pl.ds(pl.multiple_of(t * tf, tf), tf)], wf.at[s % SLOTS], wfs.at[s % SLOTS])
 
-    for s in range(SLOTS - 1):
+    for s in range(3):
         fetch_b(s).start()
         fetch_f(s).start()
 
@@ -56,9 +59,10 @@
     barrier = pltpu.get_barrier_semaphore()
     for d in range(1, R):
         pl.semaphore_signal(barrier, inc=1, device_id={"row": (r + d) % R}, device_id_type=MESH)
-    for d in range(1, C):
-        pl.semaphore_signal(barrier, inc=1, device_id={"col": (c + d) % C}, device_id_type=MESH)
-    pl.semaphore_wait(barrier, R - 1 + C - 1)
+    for d in range(1, nz):
+        pl.semaphore_signal(barrier, inc=1, device_id={"col": (z + d) % nz * 2 + me}, device_id_type=MESH)
+    pl.semaphore_signal(barrier, inc=1, device_id={"col": z * 2 + other}, device_id_type=MESH)
+    pl.semaphore_wait(barrier, R - 1 + nz)
 
     def send_g(d, k):
         return pltpu.make_async_remote_copy(
@@ -66,13 +70,20 @@
             device_id={"row": (r + d) % R}, device_id_type=MESH)
 
     def send_x(d, k):
-        return pltpu.make_async_remote_copy(
-            src_ref=lat, dst_ref=x_block(k), send_sem=las.at[d - 1], recv_sem=lar.at[d - 1],
-            device_id={"col": (c + d) % C}, device_id_type=MESH)
+        peer = z * 2 + other if d == 0 else (z + d) % nz * 2 + me
+        return pltpu.make_async_remote_copy(
+            src_ref=lat, dst_ref=x_block(k), send_sem=las.at[d], recv_sem=lar.at[d],
+            device_id={"col": peer}, device_id_type=MESH)
+
+    def relay_x(d, core):
+        k = (z + nz - d) % nz * 2 + core
+        return pltpu.make_async_remote_copy(
+            src_ref=x_block(k), dst_ref=x_block(k), send_sem=res.at[d - 1], recv_sem=rer.at[d - 1],
+            device_id={"col": z * 2 + other}, device_id_type=MESH)
 
     for d in range(1, R):
         send_g(d, r).start()
-    for d in range(1, C):
+    for d in range(nz - 1, -1, -1):
         send_x(d, c).start()
 
     gpad[:W, :] = jnp.zeros((W, co), gpad.dtype)
@@ -85,11 +96,16 @@
             src_ref=bp.at[t, other], dst_ref=pr.at[t], send_sem=prs.at[t], recv_sem=prr.at[t],
             device_id={"col": z * 2 + other}, device_id_type=MESH)
 
+    def send_mate(t):
+        return pltpu.make_async_remote_copy(
+            src_ref=bp.at[t, me, mate], dst_ref=qr.at[t], send_sem=qrs.at[t], recv_sem=qrr.at[t],
+            device_id={"col": (q * 2 + mate) * 2 + me}, device_id_type=MESH)
+
     def send_z(t, d, slot):
-        peer = (z + d) % nz
-        return pltpu.make_async_remote_copy(
-            src_ref=bp.at[t, me, peer], dst_ref=zr.at[t, slot], send_sem=zrs.at[t, d - 1],
-            recv_sem=zrr.at[t, d - 1], device_id={"col": peer * 2 + me}, device_id_type=MESH)
+        peer = (q + d) % nq
+        return pltpu.make_async_remote_copy(
+            src_ref=bp.at[t, me, zp, peer], dst_ref=zr.at[t, slot], send_sem=zrs.at[t, d - 1],
+            recv_sem=zrr.at[t, d - 1], device_id={"col": (peer * 2 + zp) * 2 + me}, device_id_type=MESH)
 
     def send_r(t, d, slot):
         peer = (r + d) % R
@@ -101,12 +117,31 @@
         send_pair(t).wait_recv()
 
         def add(k, _):
-            bp[t, me, k] = bp[t, me, k] + pr[t, k]
+            bp[t, me, k // nq, k % nq] = bp[t, me, k // nq, k % nq] + pr[t, k // nq, k % nq]
             return 0
 
         lax.fori_loop(0, nz, add, 0)
-        for d in range(1, nz):
-            send_z(t, d, z).start()
+        send_mate(t).start()
+
+    def mate_sum(t):
+        send_mate(t).wait_recv()
+
+        def add(k, _):
+            bp[t, me, zp, k] = bp[t, me, zp, k] + qr[t, k]
+            return 0
+
+        lax.fori_loop(0, nq, add, 0)
+        for d in range(1, nq):
+            send_z(t, d, q).start()
+
+    def advance(i):
+        @pl.when((i >= 1) & (i <= nb))
+        def _():
+            pair_sum(i - 1)
+
+        @pl.when((i >= 3) & (i <= nb + 2))
+        def _():
+            mate_sum(i - 3)
 
     def shifted(lo, n, first, last, cols):
         col = lax.broadcasted_iota(jnp.int32, (n, cols), 0) % W
@@ -121,20 +156,21 @@
 
     def taps(t, fetch, total, buf, dot, src, flip, cols):
         def step(kw, _):
+            s0 = t * 9 + kw * 3
+
+            @pl.when(s0 + 3 < total)
+            def _():
+                for kh in range(3):
+                    fetch(s0 + 3 + kh).start()
+
+            part = None
             for kh in range(3):
-                s = t * 9 + kw * 3 + kh
-                fetch(s).wait()
-
-                @pl.when(s + SLOTS - 1 < total)
-                def _():
-                    fetch(s + SLOTS - 1).start()
-
+                fetch(s0 + kh).wait()
+            for kh in range(3):
                 top = (2 - kh) * W if flip else kh * W
-                part = dot(src[top : top + M, :], buf[s % SLOTS])
-                if kh == 0:
-                    acc[kw, :, :cols] = part
-                else:
-                    acc[kw, :, :cols] += part
+                term = dot(src[top : top + M, :], buf[(s0 + kh) % SLOTS])
+                part = term if part is None else part + term
+            acc[kw, :, :cols] = part
             return 0
 
         lax.fori_loop(0, 3, step, 0)
@@ -143,23 +179,29 @@
         taps(t, fetch_b, nb * 9, wb, dot_nt, gpad, True, tb)
 
         def put(k, _):
-            bp[t, k % 2, k // 2] = shifted(k * cw, cw, 2, 0, tb)
+            bp[t, k % 2, k // 2 % 2, k // 4] = shifted(k * cw, cw, 2, 0, tb)
             return 0
 
         lax.fori_loop(0, C, put, 0)
         send_pair(t).start()
 
-        @pl.when(t > 0)
+        advance(t)
+
+        @pl.when(t == max(nb - 2, 0))
         def _():
-            pair_sum(t - 1)
+            for d in range(1, nz):
+                k = (z + nz - d) % nz * 2 + me
+                send_x(d, k).wait_recv()
+                relay_x(d, me).start()
 
         return 0
 
     lax.fori_loop(0, nb, back, 0)
 
     own_x.wait()
-    for d in range(1, C):
-        send_x(d, (c + C - d) % C).wait_recv()
+    send_x(0, z * 2 + other).wait_recv()
+    for d in range(1, nz):
+        relay_x(d, other).wait_recv()
 
     def fore(t, _):
         taps(t, fetch_f, nf * 9, wf, dot_nn, xpad, False, tf)
@@ -172,28 +214,33 @@
         for d in range(1, R):
             send_r(t, d, r).start()
 
-        @pl.when(t == 0)
-        def _():
-            pair_sum(nb - 1)
-
+        advance(nb + t)
         return 0
 
     lax.fori_loop(0, nf, fore, 0)
 
     for d in range(1, R):
         send_g(d, r).wait_send()
-    for d in range(1, C):
+    for i in range(nb + nf, nb + 3):
+        if i <= nb:
+            pair_sum(i - 1)
+        if i >= 3:
+            mate_sum(i - 3)
+    for d in range(nz):
         send_x(d, c).wait_send()
+    for d in range(1, nz):
+        relay_x(d, me).wait_send()
     for t in range(nb):
         send_pair(t).wait_send()
-        total = bp[t, me, z]
-        for d in range(1, nz):
-            src = (z + nz - d) % nz
+        send_mate(t).wait_send()
+        total = bp[t, me, zp, q]
+        for d in range(1, nq):
+            src = (q + nq - d) % nq
             send_z(t, d, src).wait_recv()
             total = total + zr[t, src]
         lgrad[:, t * tb : (t + 1) * tb] = total.astype(lgrad.dtype)
-        for d in range(1, nz):
-            send_z(t, d, z).wait_send()
+        for d in range(1, nq):
+            send_z(t, d, q).wait_send()
     for t in range(nf):
         total = fp[t, r]
         for d in range(1, R):
@@ -211,6 +258,7 @@
     M, rw, cw = hr * R * W, hr * W, hc * W
     tb, tf = min(512, ci), min(256, co)
     nb, nf, nz = ci // tb, co // tf, C // 2
+    nq = nz // 2
     cfg = (R, C, W, M, rw, cw, ci, co, tb, tf)
     bf, f32 = jnp.bfloat16, jnp.float32
     dma = pltpu.SemaphoreType.DMA
@@ -225,16 +273,17 @@
             pltpu.VMEM((3, M, max(tb, tf)), f32),
             pltpu.VMEM((SLOTS, tb, co), bf),
             pltpu.VMEM((SLOTS, ci, tf), bf),
-            pltpu.VMEM((nb, 2, nz, cw, tb), f32),
-            pltpu.VMEM((nb, nz, cw, tb), f32),
-            pltpu.VMEM((nb, nz, cw, tb), f32),
+            pltpu.VMEM((nb, 2, 2, nq, cw, tb), f32),
+            pltpu.VMEM((nb, 2, nq, cw, tb), f32),
+            pltpu.VMEM((nb, nq, cw, tb), f32),
+            pltpu.VMEM((nb, nq, cw, tb), f32),
             pltpu.VMEM((nf, R, rw, tf), f32),
             pltpu.VMEM((nf, R, rw, tf), f32),
             dma((SLOTS,)), dma((SLOTS,)), dma((2,)),
             dma((R - 1,)), dma((R - 1,)),
-            dma((C - 1,)), dma((C - 1,)),
-            dma((nb,)), dma((nb,)),
-            dma((nb, nz - 1)), dma((nb, nz - 1)),
+            dma((nz,)), dma((nz,)), dma((nz - 1,)), dma((nz - 1,)),
+            dma((nb,)), dma((nb,)), dma((nb,)), dma((nb,)),
+            dma((nb, nq - 1)), dma((nb, nq - 1)),
             dma((nf, R - 1)), dma((nf, R - 1)),
         ],
         compiler_params=pltpu.CompilerParams(

time: 219 us -> 145 us (0.66)
  the two profiles are of different devices: /device:TPU:9 before, /device:TPU:0 now
where the time goes in v2:
time: 145 us
  Pallas kernels  140 us (97%)
  local copies, waits for them, and re-layouts  3.75 us (3%)
    pallas_call x1, Pallas kernels, body(): pl.pallas_call(functools.partial(kernel, cfg), out_shape=(jax.ShapeDtypeS...  140 us
    unnamed x2, local copies, waits for them, and re-layouts  3.75 us

profile of v2, /device:TPU:0, one launch (start us, length us, event | category | flops | bytes accessed | tf_op | source)
XLA Modules:
  0.0 144.8 jit_solution(9768238491144464250)
XLA Ops:
  0.6 140.4 %shard_map.50 = (bf16[256,1024]{1,0:T(8,128)(2,1)}, bf16[128,2048]{1,0:T(8,128)(2,1)}) custom-call(bf16[128,2048]{1,0:T(8,128)(2,1)} %bitcast.4, bf16[3,3,2048,1024]{3,2,1,0:T(8,128)(2,1)} %ker.1, bf16[256,1024]{1,0:T(8,128)(2,1)} %bitcast.5), custom_call_target="tpu_custom_call" | custom-call | tf_op jit(solution)/shard_map/pallas_call | solution.py:265
  141.1 1.9 %copy.7 = bf16[1,8,32,1024]{3,2,1,0:T(8,128)(2,1)} copy(bf16[1,8,32,1024]{3,2,1,0:T(8,128)(2,1)} %bitcast.7) | data formatting | bytes 1048576
  143.0 1.9 %copy.8 = bf16[1,4,32,2048]{3,2,1,0:T(8,128)(2,1)} copy(bf16[1,4,32,2048]{3,2,1,0:T(8,128)(2,1)} %bitcast.6) | data formatting | bytes 1048576
